TPU v7x, 32 devices: a whole 2x2x4 slice. The times are simulated.
32 devices in a mesh: expert: 4 (over z), seq: 4 (over y, x), dp: 2 (over core).
Axes of the slice: x: 2, y: 2, z: 4, core: 2. Of those that a mesh axis runs over, the one named last changes fastest.
Arguments:
- grad_out: bfloat16 [8, 512, 2048], P(('expert', 'dp'), 'seq'), may hold values from -6 to 6
- expert_ids: int32 [8, 512, 2], P(('expert', 'dp'), 'seq'), may hold values from 0 to 3, all different within a row; in each aligned block of 128 rows (0 to 127, 128 to 255, ..., all dimensions but the last counted through in order) at most 112 rows name the same one
- gate_weights: float32 [8, 512, 2], P(('expert', 'dp'), 'seq'), may hold values from 0.1 to 0.9
- hidden: bfloat16 [8, 512, 2, 7168], P(('expert', 'dp'), 'seq'), may hold values from -0.3125 to 0.3125
- queries: bfloat16 [8, 512, 2048], P(('expert', 'dp'), 'seq')
- keys: bfloat16 [8, 512, 512], P(('expert', 'dp'), 'seq')
- values: bfloat16 [8, 512, 512], P(('expert', 'dp'), 'seq'), may hold values from -6 to 6
Outputs:
- expert_grad: bfloat16 [4, 7168, 2048], P('expert', ('seq', 'dp'))
- grad_queries: bfloat16 [8, 512, 2048], P(('expert', 'dp'), 'seq')
- grad_keys: bfloat16 [8, 512, 512], P(('expert', 'dp'), 'seq')
- grad_values: bfloat16 [8, 512, 512], P(('expert', 'dp'), 'seq')
Inputs may be any that keep to these rules, and one draw needn't show every extreme that they name: `expert_ids`: each position names two different experts; among the 128 positions of one device no expert is named more than 112 times.
All inputs are finite; a program needn't handle non-finite values.
Results may differ from a plain program's by a relative error of at most 0.018.
Values may be sent and summed in bfloat16 or wider, within the bound.
A program may use at most 128 MiB of HBM per device.

v0:
```python
import jax
import jax.numpy as jnp
from jax import lax
from jax.sharding import PartitionSpec as P

HEADS = 16
KV_HEADS = 4
HEAD_DIM = 128


def expert_grads(grad_out, expert_ids, gate_weights, hidden):
    experts = lax.axis_size("expert")
    shards = lax.axis_size("seq")
    pair_size = lax.axis_size("dp")
    tokens = grad_out.shape[1]
    model_width = grad_out.shape[2]
    unit_piece = hidden.shape[3] // shards
    owner_piece = unit_piece // pair_size
    row_count = tokens * 2
    capacity = 7 * tokens // (2 * experts)
    flat_ids = expert_ids.reshape(row_count)
    scaled = (gate_weights[0][..., None] * grad_out[0][:, None, :].astype(jnp.float32)).astype(
        jnp.bfloat16
    )
    scaled = scaled.reshape(row_count, model_width)
    onehot = (flat_ids[:, None] == jnp.arange(experts, dtype=jnp.int32)[None, :]).astype(jnp.int32)
    before = jnp.cumsum(onehot, axis=0) - onehot
    slot_index = jnp.sum(before * onehot, axis=1)
    flat_hidden = hidden.reshape(row_count, shards, unit_piece)
    hidden_send = jnp.zeros((experts, shards, capacity, unit_piece), jnp.bfloat16)
    hidden_send = hidden_send.at[flat_ids, :, slot_index, :].set(flat_hidden)
    spread = jnp.broadcast_to(scaled[:, None, :], (row_count, shards, model_width))
    grad_send = jnp.zeros((experts, shards, capacity, model_width), jnp.bfloat16)
    grad_send = grad_send.at[flat_ids, :, slot_index, :].set(spread)
    grad_recv, hidden_recv = (
        lax.all_to_all(
            grad_send.reshape(experts * shards, capacity, model_width),
            ("expert", "seq"),
            split_axis=0,
            concat_axis=0,
            tiled=True,
        ),
        lax.all_to_all(
            hidden_send.reshape(experts * shards, capacity, unit_piece),
            ("expert", "seq"),
            split_axis=0,
            concat_axis=0,
            tiled=True,
        ),
    )
    grad_rows = grad_recv.reshape(-1, model_width)
    hidden_rows = hidden_recv.reshape(-1, unit_piece)
    local_grad = lax.psum_scatter(
        lax.dot_general(
            hidden_rows, grad_rows, (((0,), (0,)), ((), ())), preferred_element_type=jnp.float32
        ).astype(jnp.bfloat16),
        "dp",
        scatter_dimension=0,
        tiled=True,
    )
    return local_grad.reshape(1, owner_piece, model_width)


def attention_grads(queries, keys, values, grad_out):
    per_group = HEADS // KV_HEADS
    score_scale = HEAD_DIM ** (-0.5)
    tokens = queries.shape[1]
    whole_keys, whole_values = (
        lax.all_gather(keys, "seq", axis=1, tiled=True),
        lax.all_gather(values, "seq", axis=1, tiled=True),
    )
    key_count = whole_keys.shape[1]
    query_heads = queries[0].reshape(tokens, KV_HEADS, per_group, HEAD_DIM)
    out_heads = grad_out[0].reshape(tokens, KV_HEADS, per_group, HEAD_DIM)
    key_heads = whole_keys[0].reshape(key_count, KV_HEADS, HEAD_DIM)
    value_heads = whole_values[0].reshape(key_count, KV_HEADS, HEAD_DIM)
    scores = (
        jnp.einsum("qhgd,khd->hgqk", query_heads, key_heads, preferred_element_type=jnp.float32)
        * score_scale
    )
    row_max = jnp.max(scores, axis=-1, keepdims=True)
    raised = jnp.exp(scores - row_max)
    probabilities = raised / jnp.sum(raised, axis=-1, keepdims=True)
    probs_low = probabilities.astype(jnp.bfloat16)
    dprobs = jnp.einsum(
        "qhgd,khd->hgqk", out_heads, value_heads, preferred_element_type=jnp.float32
    )
    row_delta = jnp.sum(probabilities * dprobs, axis=-1, keepdims=True)
    dscores = (probabilities * (dprobs - row_delta)).astype(jnp.bfloat16)
    value_part = jnp.einsum(
        "hgqk,qhgd->khd", probs_low, out_heads, preferred_element_type=jnp.float32
    )
    key_part = (
        jnp.einsum("hgqk,qhgd->khd", dscores, query_heads, preferred_element_type=jnp.float32)
        * score_scale
    )
    grad_q = (
        jnp.einsum("hgqk,khd->qhgd", dscores, key_heads, preferred_element_type=jnp.float32)
        * score_scale
    )
    key_sums, value_sums = (
        lax.psum_scatter(
            key_part.reshape(1, key_count, KV_HEADS * HEAD_DIM).astype(jnp.bfloat16),
            "seq",
            scatter_dimension=1,
            tiled=True,
        ).astype(jnp.float32),
        lax.psum_scatter(
            value_part.reshape(1, key_count, KV_HEADS * HEAD_DIM).astype(jnp.bfloat16),
            "seq",
            scatter_dimension=1,
            tiled=True,
        ).astype(jnp.float32),
    )
    grad_queries = grad_q.reshape(1, tokens, HEADS * HEAD_DIM).astype(jnp.bfloat16)
    return (grad_queries, key_sums.astype(jnp.bfloat16), value_sums.astype(jnp.bfloat16))


def on_device(grad_out, expert_ids, gate_weights, hidden, queries, keys, values):
    expert_grad = expert_grads(grad_out, expert_ids, gate_weights, hidden)
    grad_queries, grad_keys, grad_values = attention_grads(queries, keys, values, grad_out)
    return (expert_grad, grad_queries, grad_keys, grad_values)


def solution(mesh):
    in_specs = (
        P(("expert", "dp"), "seq", None),
        P(("expert", "dp"), "seq", None),
        P(("expert", "dp"), "seq", None),
        P(("expert", "dp"), "seq", None, None),
        P(("expert", "dp"), "seq", None),
        P(("expert", "dp"), "seq", None),
        P(("expert", "dp"), "seq", None),
    )
    out_specs = (
        P("expert", ("seq", "dp"), None),
        P(("expert", "dp"), "seq", None),
        P(("expert", "dp"), "seq", None),
        P(("expert", "dp"), "seq", None),
    )
    return jax.shard_map(
        on_device, mesh=mesh, in_specs=in_specs, out_specs=out_specs, check_vma=False
    )
```

profile of v0, /device:TPU:8, one launch (start us, length us, event | category | flops | bytes accessed | tf_op | source)
XLA Modules:
  0.0 442.6 jit_solution(10077372838262434562)
XLA Ops:
  7.2 0.8 copy.26
  7.9 0.1 reshape.154
  8.1 0.1 eq.29
  8.2 0.1 eq.25
  8.4 1.2 reduce-window.6
  9.6 0.1 slice.12
  9.7 0.1 copy.29
  9.8 0.1 copy.30
  9.9 0.1 add_bitcast_fusion
  10.0 9.8 %reshape.163 = bf16[256,4,1792]{2,1,0:T(4,128)(2,1)} reshape(bf16[1,128,2,7168]{3,2,1,0:T(2,128)(2,1)} %param.10) | data formatting | bytes 7340032 | tf_op jit(solution)/shard_map/reshape | solution.py:29
  19.8 4.3 broadcast_in_dim.6
  24.2 36.0 %scatter_fusion = bf16[4,4,112,1792]{3,1,2,0:T(4,128)(2,1)} fusion(bf16[4,4,112,1792]{3,1,2,0:T(4,128)(2,1)} %broadcast_in_dim.6, s32[256]{0:T(256)S(1)} %bitcast.98, bf16[256,4,1792]{2,1,0:T(4,128)(2,1)} %reshape.163), kind=kCustom, calls=%fused_computation | custom fusion | bytes 11012096 | tf_op jit(solution)/shard_map/scatter | solution.py:31
  60.2 6.3 %copy.31 = bf16[4,4,112,1792]{3,2,1,0:T(8,128)(2,1)} copy(bf16[4,4,112,1792]{3,1,2,0:T(4,128)(2,1)} %scatter_fusion) | data formatting | bytes 12845056 | tf_op jit(solution)/shard_map/scatter | solution.py:31
  66.5 0.0 copy-start.1
  66.5 7.4 %all-to-all-start = ((bf16[16,112,1792]{2,1,0:T(8,128)(2,1)}), bf16[16,112,1792]{2,1,0:T(8,128)(2,1)}, u32[]{:S(2)}, u32[]{:S(2)}) async-start(bf16[16,112,1792]{2,1,0:T(8,128)(2,1)} %bitcast.101), calls=%async_computation | async-start | bytes 12845056 | tf_op jit(solution)/shard_map/all_to_all | solution.py:43
  73.8 0.0 copy-done.1
  73.8 0.0 copy-start.7
  73.9 0.1 bitcast_convert_fusion.1
  74.0 2.5 mul.56
  76.5 2.7 mul.57
  79.2 0.0 copy-done.7
  79.2 0.1 copy.32
  79.3 0.1 mul.54
  79.4 0.2 multiply_convert_fusion
  79.6 4.2 broadcast_in_dim.8
  83.9 6.7 %broadcast_in_dim.7 = bf16[4,4,112,2048]{3,1,2,0:T(4,128)(2,1)} broadcast(bf16[]{:T(256)} %constant.7.clone.1), dimensions={} | broadcast | bytes 7340034 | tf_op jit(solution)/shard_map/broadcast_in_dim | solution.py:33
  90.6 36.3 %scatter_fusion.1 = bf16[4,4,112,2048]{3,1,2,0:T(4,128)(2,1)} fusion(bf16[4,4,112,2048]{3,1,2,0:T(4,128)(2,1)} %broadcast_in_dim.7, s32[256]{0:T(256)S(1)} %bitcast.99, bf16[256,4,2048]{2,1,0:T(4,128)(2,1)} %broadcast_in_dim.8), kind=kCustom, calls=%fused_computation.1 | custom fusion | bytes 12584960 | tf_op jit(solution)/shard_map/scatter | solution.py:34
  126.9 10.2 %copy.33 = bf16[4,4,112,2048]{3,2,1,0:T(8,128)(2,1)} copy(bf16[4,4,112,2048]{3,1,2,0:T(4,128)(2,1)} %scatter_fusion.1) | data formatting | bytes 14680064 | tf_op jit(solution)/shard_map/scatter | solution.py:34
  137.1 75.3 %all-to-all-done = bf16[16,112,1792]{2,1,0:T(8,128)(2,1)} async-done(((bf16[16,112,1792]{2,1,0:T(8,128)(2,1)}), bf16[16,112,1792]{2,1,0:T(8,128)(2,1)}, u32[]{:S(2)}, u32[]{:S(2)}) %all-to-all-start) | async-done | bytes 6422560 | tf_op jit(solution)/shard_map/all_to_all | solution.py:43
  212.4 0.0 copy-start.5
  212.4 0.0 copy-start.2
  212.4 12.8 %all-to-all-start.1 = ((bf16[16,112,2048]{2,1,0:T(8,128)(2,1)}), bf16[16,112,2048]{2,1,0:T(8,128)(2,1)}, u32[]{:S(2)}, u32[]{:S(2)}) async-start(bf16[16,112,2048]{2,1,0:T(8,128)(2,1)} %bitcast.100), calls=%async_computation.1 | async-start | bytes 14680064 | tf_op jit(solution)/shard_map/all_to_all | solution.py:36
  225.2 0.0 reduce-scatter.6.cloned.1.call-start
  225.2 0.3 copy.61
  225.5 0.0 copy-done.5
  225.5 0.1 copy.34
  225.7 0.0 copy-done.2
  225.7 0.3 copy.60
  226.0 0.0 copy-done.6
  226.0 0.0 copy-start.3
  226.0 0.1 copy.37
  226.1 40.8 %all_gather.6 = bf16[1,512,512]{1,2,0:T(8,128)(2,1)S(1)} all-gather(bf16[1,128,512]{1,2,0:T(8,128)(2,1)S(1)} %copy.34), channel_id=1, replica_groups=mesh['expert'=4,'seq'=4,'dp'=2] {'seq'}, dimensions={1}, use_global_device_ids=true | all-gather | bytes 655360 | tf_op jit(solution)/shard_map/all_gather | solution.py:69
  266.9 39.5 %all_gather.7 = bf16[1,512,512]{1,2,0:T(8,128)(2,1)S(1)} all-gather(bf16[1,128,512]{1,2,0:T(8,128)(2,1)S(1)} %copy.37), channel_id=1, replica_groups=mesh['expert'=4,'seq'=4,'dp'=2] {'seq'}, dimensions={1}, use_global_device_ids=true | all-gather | bytes 655360 | tf_op jit(solution)/shard_map/all_gather | solution.py:70
  306.5 3.4 fusion.28
  309.9 3.1 fusion.1
  313.0 0.0 copy-done.3
  313.0 0.3 copy-done
  313.3 0.7 fusion.3
  314.1 0.3 copy-done.4
  314.4 1.6 fusion.16
  316.0 2.1 copy.43
  318.1 0.0 reduce-scatter.6.cloned.1.call-update
  318.1 0.0 reduce-scatter.8.cloned.1.call-start
  318.2 3.8 fusion.18
  322.0 2.1 copy.46
  324.0 0.0 reduce-scatter.8.cloned.1.call-update
  324.0 0.0 reduce-scatter.4.cloned.1.call-start
  324.1 58.2 %all-to-all-done.1 = bf16[16,112,2048]{2,1,0:T(8,128)(2,1)} async-done(((bf16[16,112,2048]{2,1,0:T(8,128)(2,1)}), bf16[16,112,2048]{2,1,0:T(8,128)(2,1)}, u32[]{:S(2)}, u32[]{:S(2)}) %all-to-all-start.1) | async-done | bytes 7340064 | tf_op jit(solution)/shard_map/all_to_all | solution.py:36
  382.3 19.6 %bitcast_convert_fusion = bf16[1792,2048]{1,0:T(8,128)(2,1)} fusion(bf16[16,112,1792]{2,1,0:T(8,128)(2,1)} %all-to-all-done, bf16[16,112,2048]{2,1,0:T(8,128)(2,1)} %all-to-all-done.1), kind=kOutput, calls=%fused_computation.3 | convolution fusion | flops 13157007360 | bytes 21102592 | tf_op jit(solution)/shard_map/dot_general | solution.py:54
  401.9 0.0 reduce-scatter.4.cloned.1.call-update
  402.0 0.5 fusion.17
  402.5 1.0 copy.47
  403.5 13.6 %reduce-scatter.8.cloned.1.call-done = bf16[1,128,512]{2,1,0:T(8,128)(2,1)} async-done(((bf16[1,512,512]{2,1,0:T(8,128)(2,1)}), bf16[1,128,512]{2,1,0:T(8,128)(2,1)}) %reduce-scatter.8.cloned.1.call-update) | async-done | bytes 131088 | tf_op jit(solution)/shard_map/reduce_scatter | solution.py:108
  417.1 19.0 %reduce-scatter.4.cloned.1.call-done = bf16[896,2048]{1,0:T(8,128)(2,1)} async-done(((bf16[1792,2048]{1,0:T(8,128)(2,1)}), bf16[896,2048]{1,0:T(8,128)(2,1)}) %reduce-scatter.4.cloned.1.call-update) | async-done | bytes 3670032 | tf_op jit(solution)/shard_map/reduce_scatter | solution.py:53
  (9 shorter events, 0.1 us)
Async XLA Ops:
  66.5 7.4 %copy-start.1 = (bf16[1,128,2048]{2,1,0:T(8,128)(2,1)S(1)}, bf16[1,128,2048]{2,1,0:T(8,128)(2,1)}, u32[]{:S(2)}) copy-start(bf16[1,128,2048]{2,1,0:T(8,128)(2,1)} %param.7) | copy-start | bytes 1572868
  66.5 145.9 %all-to-all-start = ((bf16[16,112,1792]{2,1,0:T(8,128)(2,1)}), bf16[16,112,1792]{2,1,0:T(8,128)(2,1)}, u32[]{:S(2)}, u32[]{:S(2)}) async-start(bf16[16,112,1792]{2,1,0:T(8,128)(2,1)} %bitcast.101), calls=%async_computation | async-start | bytes 12845056 | tf_op jit(solution)/shard_map/all_to_all | solution.py:43
  73.8 5.3 %copy-start.7 = (f32[1,128,2]{1,2,0:T(2,128)S(1)}, f32[1,128,2]{1,2,0:T(2,128)}, u32[]{:S(2)}) copy-start(f32[1,128,2]{1,2,0:T(2,128)} %param.9) | copy-start | bytes 3076
  212.4 13.1 %copy-start.5 = (bf16[1,128,512]{2,1,0:T(8,128)(2,1)S(1)}, bf16[1,128,512]{2,1,0:T(8,128)(2,1)}, u32[]{:S(2)}) copy-start(bf16[1,128,512]{2,1,0:T(8,128)(2,1)} %param.12) | copy-start | bytes 393220
  212.4 13.2 %copy-start.2 = (bf16[1,128,2048]{2,1,0:T(8,128)(2,1)S(1)}, bf16[1,128,2048]{2,1,0:T(8,128)(2,1)}, u32[]{:S(2)}) copy-start(bf16[1,128,2048]{2,1,0:T(8,128)(2,1)} %param.11) | copy-start | bytes 1572868
  212.4 13.5 %copy-start.6 = (bf16[1,128,512]{2,1,0:T(8,128)(2,1)S(1)}, bf16[1,128,512]{2,1,0:T(8,128)(2,1)}, u32[]{:S(2)}) copy-start(bf16[1,128,512]{2,1,0:T(8,128)(2,1)} %param.13) | copy-start | bytes 393220
  212.4 169.9 %all-to-all-start.1 = ((bf16[16,112,2048]{2,1,0:T(8,128)(2,1)}), bf16[16,112,2048]{2,1,0:T(8,128)(2,1)}, u32[]{:S(2)}, u32[]{:S(2)}) async-start(bf16[16,112,2048]{2,1,0:T(8,128)(2,1)} %bitcast.100), calls=%async_computation.1 | async-start | bytes 14680064 | tf_op jit(solution)/shard_map/all_to_all | solution.py:36
  225.2 178.3 %reduce-scatter.6.cloned.1.call-start = ((), (), s32[]{:S(2)}) async-start(), calls=%async_computation.6 | async-start | bytes 655360 | tf_op jit(solution)/shard_map/reduce_scatter | solution.py:102
  226.0 87.1 %copy-start.3 = (bf16[1,128,2048]{1,2,0:T(8,128)(2,1)}, bf16[1,128,2048]{1,2,0:T(8,128)(2,1)S(1)}, u32[]{:S(2)}) copy-start(bf16[1,128,2048]{1,2,0:T(8,128)(2,1)S(1)} %copy.60) | copy-start | bytes 1572868
  309.9 3.4 copy-start
  313.3 1.0 copy-start.4
  318.1 99.0 %reduce-scatter.8.cloned.1.call-start = ((), (), s32[]{:S(2)}) async-start(), calls=%async_computation.7 | async-start | bytes 655360 | tf_op jit(solution)/shard_map/reduce_scatter | solution.py:108
  324.0 112.0 %reduce-scatter.4.cloned.1.call-start = ((), (), s32[]{:S(2)}) async-start(), calls=%async_computation.5 | async-start | bytes 11010048 | tf_op jit(solution)/shard_map/reduce_scatter | solution.py:53
Sparse Core Ops, SparseCore 0:
  318.2 70.8 reduce-scatter.5
  392.8 24.2 reduce-scatter.7
  420.0 16.0 reduce-scatter.3
where the time goes:
time: 446 us; the launch traced here: 443 us
  waiting for transfers between devices  166 us (37%)
  local copies, waits for them, and re-layouts  127 us (28%)
  blocking collectives  80.3 us (18%)
  matrix products  32.1 us (7%)
  starting transfers between devices  20.2 us (5%)
  between operations  13.9 us (3%)
    all_to_all x1, waiting for transfers between devices, expert_grads(): lax.all_to_all(hidden_send.reshape(experts * shards, capacity, unit_piece...  75.3 us
    all_to_all x1, waiting for transfers between devices, expert_grads(): lax.all_to_all(grad_send.reshape(experts * shards, capacity, model_width)...  58.2 us
    scatter x2, local copies, waits for them, and re-layouts, expert_grads(): grad_send = grad_send.at[flat_ids, :, slot_index, :].set(spread)  46.5 us
    scatter x2, local copies, waits for them, and re-layouts, expert_grads(): hidden_send = hidden_send.at[flat_ids, :, slot_index, :].set(flat_hidden)  42.3 us
    all_gather x1, blocking collectives, attention_grads(): lax.all_gather(keys, 'seq', axis=1, tiled=True)  40.8 us
    all_gather x1, blocking collectives, attention_grads(): lax.all_gather(values, 'seq', axis=1, tiled=True)  39.5 us
    dot_general x1, matrix products, expert_grads(): lax.dot_general(hidden_rows, grad_rows, (((0,), (0,)), ((), ())), preferr...  19.6 us
    reduce_scatter x1, waiting for transfers between devices, expert_grads(): lax.psum_scatter(lax.dot_general(hidden_rows, grad_rows, (((0,), (0,)), (...  19 us
  transfers between devices with their start and end apart: 5, of which 4 were waited for; matrix products, arithmetic and copies ran while one was open for 23% of the time, Pallas kernels for 0%

commit v1 on v0

v1 whole, which is shorter than its diff:
```python
import functools

import jax
import jax.numpy as jnp
from jax import lax
from jax.experimental import pallas as pl
from jax.experimental.pallas import tpu as pltpu
from jax.sharding import PartitionSpec as P

HEADS = 16
KV_HEADS = 4
HEAD_DIM = 128
GROUP = HEADS // KV_HEADS
MESH = pl.DeviceIdType.MESH


def dot(a, b, contract):
    return lax.dot_general(a, b, (contract, ((), ())), preferred_element_type=jnp.float32)


def routing_codes(ids, order_row, order_col, experts, capacity):
    count = max(8, experts)
    rows = ids.shape[1]
    expert_of = lax.broadcasted_iota(jnp.int32, (count, rows), 0).astype(jnp.float32)
    onehot = (expert_of == ids).astype(jnp.float32)
    earlier = (order_col < order_row).astype(jnp.float32)
    before = dot(onehot.astype(jnp.bfloat16), earlier.astype(jnp.bfloat16), ((1,), (0,)))
    slot = jnp.sum(before * onehot, axis=0, keepdims=True)
    return ids * float(capacity) + slot


def kernel(
    dims,
    ids_t, ids_k, gates_k, go, q, k, v, hid,
    eg_out, gq_out, gk_out, gv_out,
    kbuf, vbuf, idbuf, hraw, hsend, hrecv, gsend, grecv,
    kpart, vpart, kown, vown, kin, vin, precv,
    small_send, small_recv, local_sem, hraw_send, hraw_recv,
    gz_send, gz_recv, gs_send, gs_recv, hz_send, hz_recv,
    part_send, part_recv, pair_send, pair_recv,
):
    E, S, T, C, U, D = dims
    half = U // 2
    e = lax.axis_index("expert")
    s = lax.axis_index("seq")
    d = lax.axis_index("dp")
    seq_peer = [lax.rem(s + i, S) for i in range(S)]

    def ex_peer(j):
        return lax.rem(e + j, E)

    barrier = pltpu.get_barrier_semaphore()
    for i in range(1, S):
        pl.semaphore_signal(barrier, inc=1, device_id={"seq": seq_peer[i]}, device_id_type=MESH)

    @pl.loop(1, E)
    def _(j):
        pl.semaphore_signal(barrier, inc=1, device_id={"expert": ex_peer(j)}, device_id_type=MESH)

    pl.semaphore_signal(barrier, inc=1, device_id={"dp": 1 - d}, device_id_type=MESH)
    pl.semaphore_wait(barrier, S + E - 1)

    def send(src, dst, ssem, rsem, where):
        return pltpu.make_async_remote_copy(
            src_ref=src, dst_ref=dst, send_sem=ssem, recv_sem=rsem,
            device_id=where, device_id_type=MESH,
        )

    def small_copy(n, i, slot):
        src, dst = ((ids_t, idbuf), (k, kbuf), (v, vbuf))[n]
        return send(src, dst.at[slot], small_send.at[n, i], small_recv.at[n, slot], {"seq": seq_peer[i]})

    def raw_copy(i, slot):
        cols = pl.ds(pl.multiple_of(seq_peer[i] * U, 128), U)
        return send(hid.at[:, cols], hraw.at[slot], hraw_send.at[i], hraw_recv.at[slot], {"seq": seq_peer[i]})

    own_cols = pl.ds(pl.multiple_of(s * U, 128), U)
    own_raw = pltpu.make_async_copy(hid.at[:, own_cols], hraw.at[s], local_sem.at[0])
    own_raw.start()
    for i in range(1, S):
        for n in range(3):
            small_copy(n, i, s).start()
    for i in range(1, S):
        raw_copy(i, s).start()
    kbuf[s] = k[...]
    vbuf[s] = v[...]
    idbuf[s] = ids_t[...]

    rows = 2 * T
    col = lax.broadcasted_iota(jnp.int32, (rows, rows), 1)
    row = lax.broadcasted_iota(jnp.int32, (rows, rows), 0)
    code = routing_codes(
        ids_k[0:1, :], 2 * lax.rem(col, T) + col // T, 2 * lax.rem(row, T) + row // T, E, C
    )
    place = lax.broadcasted_iota(jnp.int32, (E * C, rows), 0).astype(jnp.float32)
    picks = (place == code).astype(jnp.float32)
    gate = jnp.sum(picks * gates_k[0:1, :], axis=1, keepdims=True)
    token_picks = (picks[:, :T] + picks[:, T:]).astype(jnp.bfloat16)
    gsend[...] = (dot(token_picks, go[...], ((1,), (0,))) * gate).astype(jnp.bfloat16)

    def expert_rows(p):
        return pl.ds(pl.multiple_of(p * C, 16), C)

    def gz_copy(j, slot):
        p = ex_peer(j)
        return send(gsend.at[expert_rows(p)], grecv.at[s, slot], gz_send.at[j], gz_recv.at[slot], {"expert": p})

    def gs_copy(i, z, slot):
        return send(grecv.at[s, z], grecv.at[slot, z], gs_send.at[i, z], gs_recv.at[slot, z], {"seq": seq_peer[i]})

    def gs_wait(i, z):
        slot = seq_peer[i]
        send(grecv.at[s, z], grecv.at[slot, z], gs_send.at[i, z], gs_recv.at[slot, z], {"seq": slot}).wait_recv()

    @pl.loop(1, E)
    def _(j):
        gz_copy(j, e).start()

    grecv[s, e] = gsend[expert_rows(e)]
    for i in range(1, S):
        gs_copy(i, e, s).start()

    def hz_copy(i, j, slot):
        p = ex_peer(j)
        src = seq_peer[i]
        return send(hsend.at[src, expert_rows(p)], hrecv.at[src, slot], hz_send.at[src, j], hz_recv.at[src, slot], {"expert": p})

    def pack_hidden(i):
        src = seq_peer[i]
        hcode = routing_codes(idbuf[src, 0:1, :], col, row, E, C)
        hpicks = (place == hcode).astype(jnp.bfloat16)
        for u0 in range(0, U, half):
            hsend[src, :, u0 : u0 + half] = dot(
                hpicks, hraw[src, :, u0 : u0 + half], ((1,), (0,))
            ).astype(jnp.bfloat16)

        @pl.loop(1, E)
        def _(j):
            hz_copy(i, j, e).start()

        hrecv[src, e] = hsend[src, expert_rows(e)]

    own_raw.wait()
    pack_hidden(0)

    scale = HEAD_DIM ** (-0.5)
    length = S * T

    def attention(j):
        lanes = slice(j * HEAD_DIM, (j + 1) * HEAD_DIM)
        heads = [slice(h * HEAD_DIM, (h + 1) * HEAD_DIM) for h in range(j * GROUP, (j + 1) * GROUP)]
        qs = jnp.concatenate([q[:, h] for h in heads], axis=0)
        gs = jnp.concatenate([go[:, h] for h in heads], axis=0)
        kj = kbuf[:, :, lanes].reshape(length, HEAD_DIM)
        vj = vbuf[:, :, lanes].reshape(length, HEAD_DIM)
        scores = dot(qs, kj, ((1,), (1,))) * scale
        raised = jnp.exp(scores - jnp.max(scores, axis=-1, keepdims=True))
        probs = raised / jnp.sum(raised, axis=-1, keepdims=True)
        dprobs = dot(gs, vj, ((1,), (1,)))
        delta = jnp.sum(probs * dprobs, axis=-1, keepdims=True)
        ds = (probs * (dprobs - delta)).astype(jnp.bfloat16)
        dv = dot(probs.astype(jnp.bfloat16), gs, ((0,), (0,)))
        dk = dot(ds, qs, ((0,), (0,))) * scale
        dq = dot(ds, kj, ((1,), (0,))) * scale
        for n, h in enumerate(heads):
            gq_out[:, h] = dq[n * T : (n + 1) * T].astype(jnp.bfloat16)
        dk = dk.reshape(S, T, HEAD_DIM)
        dv = dv.reshape(S, T, HEAD_DIM)
        kown[:, :, lanes] = dk
        vown[:, :, lanes] = dv
        kpart[:, :, lanes] = dk.astype(jnp.bfloat16)
        vpart[:, :, lanes] = dv.astype(jnp.bfloat16)

    for i in range(1, S):
        for n in range(3):
            small_copy(n, i, seq_peer[i]).wait_recv()

    attention(0)

    @pl.loop(1, E)
    def _(j):
        z = ex_peer(j)
        gz_copy(j, z).wait_recv()
        for i in range(1, S):
            gs_copy(i, z, s).start()

    attention(1)
    for i in range(1, S):
        raw_copy(i, seq_peer[i]).wait_recv()
        pack_hidden(i)
        if i + 1 < KV_HEADS:
            attention(i + 1)
    for j in range(S, KV_HEADS):
        attention(j)

    def part_copy(n, i, slot):
        src, dst = ((kpart, kin), (vpart, vin))[n]
        return send(src.at[seq_peer[i]], dst.at[slot], part_send.at[n, i], part_recv.at[n, slot], {"seq": seq_peer[i]})

    for i in range(1, S):
        for n in range(2):
            part_copy(n, i, s).start()
    for n, (own, got, out) in enumerate(((kown, kin, gk_out), (vown, vin, gv_out))):
        total = own[s]
        for i in range(1, S):
            part_copy(n, i, seq_peer[i]).wait_recv()
            total = total + got[seq_peer[i]].astype(jnp.float32)
        out[...] = total.astype(jnp.bfloat16)

    @pl.loop(1, E)
    def _(j):
        for i in range(S):
            hz_copy(i, j, ex_peer(j)).wait_recv()

    @pl.loop(0, E)
    def _(z):
        for i in range(1, S):
            gs_wait(i, z)

    wide = 256
    tiles = [(o, min(wide, half - o)) for o in range(0, half, wide)]

    def product(base, off, width):
        units = pl.ds(pl.multiple_of(base + off, 128), width)
        h = hrecv[:, :, :, units].reshape(S * E * C, width)
        return dot(h, grecv[...].reshape(S * E * C, D), ((0,), (0,)))

    def pair_copy(n):
        off, width = tiles[n]
        return send(eg_out.at[off : off + width], precv.at[off : off + width], pair_send.at[n], pair_recv.at[n], {"dp": 1 - d})

    for n, (off, width) in enumerate(tiles):
        eg_out[off : off + width, :] = product((1 - d) * half, off, width).astype(jnp.bfloat16)
        pair_copy(n).start()
    for n, (off, width) in enumerate(tiles):
        mine = product(d * half, off, width)
        pair_copy(n).wait_recv()
        pair_copy(n).wait_send()
        got = precv[off : off + width, :].astype(jnp.float32)
        eg_out[off : off + width, :] = (mine + got).astype(jnp.bfloat16)

    for i in range(1, S):
        for n in range(3):
            small_copy(n, i, s).wait_send()
        for n in range(2):
            part_copy(n, i, s).wait_send()
        raw_copy(i, s).wait_send()

    @pl.loop(0, E)
    def _(z):
        for i in range(1, S):
            gs_copy(i, z, s).wait_send()

    @pl.loop(1, E)
    def _(j):
        gz_copy(j, e).wait_send()
        for i in range(S):
            hz_copy(i, j, e).wait_send()


def on_device(grad_out, expert_ids, gate_weights, hidden, queries, keys, values):
    E = lax.axis_size("expert")
    S = lax.axis_size("seq")
    T = grad_out.shape[1]
    D = grad_out.shape[2]
    U = hidden.shape[3] // S
    C = -(-(7 * T // (2 * E)) // 16) * 16
    KD = keys.shape[2]
    rows = 2 * T
    bf, f32 = jnp.bfloat16, jnp.float32
    ids = expert_ids[0].astype(f32)
    ids_t = jnp.broadcast_to(ids.reshape(1, rows), (8, rows))
    ids_k = jnp.broadcast_to(ids.T.reshape(1, rows), (8, rows))
    gates_k = jnp.broadcast_to(gate_weights[0].T.reshape(1, rows), (8, rows))
    tiles = -(-(U // 2) // 256)
    vm = pl.BlockSpec(memory_space=pltpu.VMEM)
    dma = pltpu.SemaphoreType.DMA
    eg, gq, gk, gv = pl.pallas_call(
        functools.partial(kernel, (E, S, T, C, U, D)),
        out_shape=(
            jax.ShapeDtypeStruct((U // 2, D), bf),
            jax.ShapeDtypeStruct((T, queries.shape[2]), bf),
            jax.ShapeDtypeStruct((T, KD), bf),
            jax.ShapeDtypeStruct((T, KD), bf),
        ),
        in_specs=[vm] * 7 + [pl.BlockSpec(memory_space=pl.ANY)],
        out_specs=(vm,) * 4,
        scratch_shapes=[
            pltpu.VMEM((S, T, KD), bf),
            pltpu.VMEM((S, T, KD), bf),
            pltpu.VMEM((S, 8, rows), f32),
            pltpu.VMEM((S, rows, U), bf),
            pltpu.VMEM((S, E * C, U), bf),
            pltpu.VMEM((S, E, C, U), bf),
            pltpu.VMEM((E * C, D), bf),
            pltpu.VMEM((S, E, C, D), bf),
            pltpu.VMEM((S, T, KD), bf),
            pltpu.VMEM((S, T, KD), bf),
            pltpu.VMEM((S, T, KD), f32),
            pltpu.VMEM((S, T, KD), f32),
            pltpu.VMEM((S, T, KD), bf),
            pltpu.VMEM((S, T, KD), bf),
            pltpu.VMEM((U // 2, D), bf),
            dma((3, S)), dma((3, S)), dma((1,)), dma((S,)), dma((S,)),
            dma((E,)), dma((E,)), dma((S, E)), dma((S, E)), dma((S, E)), dma((S, E)),
            dma((2, S)), dma((2, S)), dma((tiles,)), dma((tiles,)),
        ],
        compiler_params=pltpu.CompilerParams(
            collective_id=0, has_side_effects=True, vmem_limit_bytes=60 * 1024 * 1024
        ),
    )(ids_t, ids_k, gates_k, grad_out[0], queries[0], keys[0], values[0], hidden.reshape(rows, S * U))
    return (eg[None], gq[None], gk[None], gv[None])


def solution(mesh):
    split = P(("expert", "dp"), "seq", None)
    in_specs = (split, split, split, P(("expert", "dp"), "seq", None, None), split, split, split)
    out_specs = (P("expert", ("seq", "dp"), None), split, split, split)
    return jax.shard_map(
        on_device, mesh=mesh, in_specs=in_specs, out_specs=out_specs, check_vma=False
    )
```

time: 446 us -> 224 us (0.50)
  Pallas kernels: 0 us -> 204 us
  waiting for transfers between devices: 166 us -> 0 us
  local copies, waits for them, and re-layouts: 127 us -> 17.7 us
  blocking collectives: 80.3 us -> 0 us
  matrix products: 32.1 us -> 0 us
  starting transfers between devices: 20.2 us -> 0 us
  between operations: 13.9 us -> 0.67 us
    pallas_call x0 -> x1, Pallas kernels: none -> 204 us  [on_device(): pl.pallas_call(functools.partial(kernel, (E, S, T, C, U, D)), out_shape=(...]
    all_to_all x2 -> x0, waiting for transfers between devices: 134 us -> none  [the longest x1 75.3 us: expert_grads(): lax.all_to_all(hidden_send.reshape(experts * shards, capacity, unit_piece...]
    scatter x4 -> x0, local copies, waits for them, and re-layouts: 88.8 us -> none  [the longest x2 46.5 us: expert_grads(): grad_send = grad_send.at[flat_ids, :, slot_index, :].set(spread)]
    all_gather x2 -> x0, blocking collectives: 80.3 us -> none  [the longest x1 40.8 us: attention_grads(): lax.all_gather(keys, 'seq', axis=1, tiled=True)]
    reduce_scatter x3 -> x0, waiting for transfers between devices: 32.6 us -> none  [the longest x1 19 us: expert_grads(): lax.psum_scatter(lax.dot_general(hidden_rows, grad_rows, (((0,), (0,)), (...]
    dot_general x5 -> x0, matrix products: 28.6 us -> none  [the longest x1 19.6 us: expert_grads(): lax.dot_general(hidden_rows, grad_rows, (((0,), (0,)), ((), ())), preferr...]
    all_to_all x2 -> x0, starting transfers between devices: 20.1 us -> none  [the longest x1 12.8 us: expert_grads(): lax.all_to_all(grad_send.reshape(experts * shards, capacity, model_width)...]
    broadcast_in_dim x3, local copies, waits for them, and re-layouts: 15.3 us -> 2.49 us  [the longest x1 1.28 us: on_device(): gates_k = jnp.broadcast_to(gate_weights[0].T.reshape(1, rows), (8, rows))]
  transfers between devices with their start and end apart: 5 -> 0, of which waited for: 4 -> 0; matrix products, arithmetic and copies ran while one was open for 23% -> 0% of each run, Pallas kernels for 0% -> 0%
where the time goes in v1:
time: 224 us; the launch traced here: 223 us
  Pallas kernels  204 us (91%)
  local copies, waits for them, and re-layouts  17.7 us (8%)
    pallas_call x1, Pallas kernels, on_device(): pl.pallas_call(functools.partial(kernel, (E, S, T, C, U, D)), out_shape=(...  204 us
    reshape x1, local copies, waits for them, and re-layouts, on_device(): hidden.reshape(rows, S * U)  8.38 us
    unnamed x10, local copies, waits for them, and re-layouts  6.56 us

profile of v1, /device:TPU:8, one launch (start us, length us, event | category | flops | bytes accessed | tf_op | source)
XLA Modules:
  0.0 223.2 jit_solution(1830560617808800766)
XLA Ops:
  0.6 0.7 convert_bitcast_fusion
  1.3 0.6 broadcast_in_dim.33.ids_k
  1.9 1.3 broadcast_in_dim.35.gates_k
  3.2 0.1 copy.11
  3.3 0.1 convert_element_type.14
  3.4 0.6 broadcast_in_dim.31.ids_t
  4.1 8.4 %reshape.23.hid = bf16[256,7168]{1,0:T(8,128)(2,1)} reshape(bf16[1,128,2,7168]{3,2,1,0:T(2,128)(2,1)} %param.10) | data formatting | bytes 7340032 | tf_op jit(solution)/shard_map/reshape | solution.py:311
  12.4 204.2 %shard_map.102 = (bf16[896,2048]{1,0:T(8,128)(2,1)}, bf16[128,2048]{1,0:T(8,128)(2,1)}, bf16[128,512]{1,0:T(8,128)(2,1)}, bf16[128,512]{1,0:T(8,128)(2,1)}) custom-call(f32[8,256]{1,0:T(8,128)} %broadcast_in_dim.31.ids_t, f32[8,256]{1,0:T(8,128)} %broadcast_in_dim.33.ids_k, f32[8,256]{1,0:T(8,128)} %broadcast_in_dim.35.gates_k, bf16[128,2048]{1,0:T(8,128)(2,1)} %bitcast.20, ...), custom_call_target="tpu_custom_call" | custom-call | tf_op jit(solution)/shard_map/pallas_call | solution.py:278
  216.6 0.0 copy-start
  216.7 0.0 copy-start.2
  216.7 0.0 copy-start.1
  216.7 4.4 %copy.16 = bf16[1,896,2048]{2,1,0:T(8,128)(2,1)} copy(bf16[1,896,2048]{2,1,0:T(8,128)(2,1)} %bitcast.19) | data formatting | bytes 7340032
  221.1 0.0 copy-done
  221.1 0.8 copy.17
  221.9 0.0 copy-done.2
  221.9 0.7 copy.18
  222.6 0.0 copy-done.1
  222.6 0.7 copy.19
Async XLA Ops:
  216.6 4.5 %copy-start = (bf16[128,2048]{1,0:T(8,128)(2,1)S(1)}, bf16[128,2048]{1,0:T(8,128)(2,1)}, u32[]{:S(2)}) copy-start(bf16[128,2048]{1,0:T(8,128)(2,1)} %get-tuple-element.9) | copy-start | bytes 1572868
  216.7 5.3 %copy-start.2 = (bf16[128,512]{1,0:T(8,128)(2,1)S(1)}, bf16[128,512]{1,0:T(8,128)(2,1)}, u32[]{:S(2)}) copy-start(bf16[128,512]{1,0:T(8,128)(2,1)} %get-tuple-element.10) | copy-start | bytes 393220
  216.7 5.9 %copy-start.1 = (bf16[128,512]{1,0:T(8,128)(2,1)S(1)}, bf16[128,512]{1,0:T(8,128)(2,1)}, u32[]{:S(2)}) copy-start(bf16[128,512]{1,0:T(8,128)(2,1)} %get-tuple-element.11) | copy-start | bytes 393220
